TPU v7x, 256 devices: a whole 4x4x8 slice. The times are simulated.
256 devices in a mesh: loop: 32 (over z, x_hi, core), grp: 8 (over y, x_lo).
Axes of the slice: x: 4 (x_hi: 2, x_lo: 2; x = x_hi * 2 + x_lo), y: 4, z: 8, core: 2. Of those that a mesh axis runs over, the one named last changes fastest.
Arguments:
- node_feats: bfloat16 [512, 65536], P(None, ('loop', 'grp')), may hold values from -6 to 6
- tile_vals: bfloat16 [32, 32, 10, 128, 128], P('loop'), may hold values from -0.375 to 0.375
- tile_rows: int32 [32, 32, 10], P('loop'), may hold values from 0 to 15
- tile_cols: int32 [32, 32, 10], P('loop'), may hold values from 0 to 15
- tile_count: int32 [32, 32], P('loop'), may hold values from 0 to 10, as said below
- degree: int32 [65536], P('loop'), may hold values from 1 to 8
- w_self: bfloat16 [512, 512], replicated, may hold values from -0.25 to 0.25
- w_neigh: bfloat16 [512, 512], replicated, may hold values from -0.25 to 0.25
Outputs:
- node_out: bfloat16 [512, 65536], P(None, ('loop', 'grp'))
Inputs may be any that keep to these rules, and one draw needn't show every extreme that they name: Only the first tile_count[j, t] slots of a pair are tiles of the graph; later slots hold values that belong to no edge. Some pair uses all 10 slots in every draw.
All inputs are finite; a program needn't handle non-finite values.
Results may differ from a plain program's by a relative error of at most 0.0035.
Values may be sent and summed in bfloat16 or wider, within the bound.
No kernel may reach another device: no remote copies, remote signals or barrier semaphores. Data moves between devices by JAX's collectives and lax.ppermute only.
A program may use at most 64 MiB of HBM per device.

v0:
```python
import jax
import jax.numpy as jnp
from jax import lax
from jax.sharding import PartitionSpec as P


def from_behind(shard, axis, by):
    size = lax.axis_size(axis)
    return lax.ppermute(shard, axis, [(i, (i + by) % size) for i in range(size)])


def tile_terms(sources, tiles, row_ids, col_ids, filled):
    channels = sources.shape[0]
    tile_edge = tiles.shape[-1]
    slot_count = tiles.shape[0]
    block_count = sources.shape[1] // tile_edge
    grouped = sources.reshape(channels, block_count, tile_edge)
    block_ids = lax.iota(jnp.int32, block_count)
    picker = (col_ids[:, None] == block_ids[None, :]).astype(jnp.bfloat16)
    chosen = jnp.einsum("kb,fbc->kfc", picker, grouped, preferred_element_type=jnp.float32).astype(
        jnp.bfloat16
    )
    products = jnp.einsum("kfc,krc->kfr", chosen, tiles, preferred_element_type=jnp.float32)
    active = lax.iota(jnp.int32, slot_count) < filled
    placer = ((row_ids[:, None] == block_ids[None, :]) & active[:, None]).astype(jnp.float32)
    spread = jnp.einsum(
        "kb,kfr->fbr",
        placer,
        products,
        precision=lax.Precision.HIGHEST,
        preferred_element_type=jnp.float32,
    )
    return spread.reshape(channels, block_count * tile_edge)


def project(weight, features):
    return lax.dot_general(
        weight, features, (((0,), (0,)), ((), ())), preferred_element_type=jnp.float32
    )


def shards(node_feats, tile_vals, tile_rows, tile_cols, tile_count, degree, w_self, w_neigh):
    cycle_size = lax.axis_size("loop")
    position = lax.axis_index("loop")
    columns = lax.all_to_all(node_feats, "grp", split_axis=0, concat_axis=1, tiled=True)
    own_tiles = tile_vals[0]
    own_rows = tile_rows[0]
    own_cols = tile_cols[0]
    own_counts = tile_count[0]

    def contribution(target):
        return tile_terms(
            columns,
            lax.dynamic_index_in_dim(own_tiles, target, 0, False),
            lax.dynamic_index_in_dim(own_rows, target, 0, False),
            lax.dynamic_index_in_dim(own_cols, target, 0, False),
            lax.dynamic_index_in_dim(own_counts, target, 0, False),
        )

    initial = contribution((position + 1) % cycle_size)

    def advance(offset, partial_value):
        arrived = from_behind(partial_value, "loop", -1)
        return arrived + contribution((position + offset + 1) % cycle_size)

    summed = lax.fori_loop(1, cycle_size, advance, initial)
    neighbor = (summed / degree.astype(jnp.float32)[None, :]).astype(jnp.bfloat16)
    node_major = lax.all_to_all(neighbor, "grp", split_axis=1, concat_axis=0, tiled=True)
    combined = project(w_self, node_feats) + project(w_neigh, node_major)
    hidden = jnp.maximum(combined, 0.0)
    mean_square = jnp.mean(hidden * hidden, axis=0, keepdims=True)
    return (hidden * lax.rsqrt(mean_square + 1e-05)).astype(jnp.bfloat16)


def solution(mesh):
    return jax.shard_map(
        shards,
        mesh=mesh,
        in_specs=(
            P(None, ("loop", "grp")),
            P("loop", None, None, None, None),
            P("loop", None, None),
            P("loop", None, None),
            P("loop", None),
            P("loop"),
            P(),
            P(),
        ),
        out_specs=P(None, ("loop", "grp")),
        check_vma=False,
    )
```

profile of v0, /device:TPU:2, one launch (start us, length us, event | category | flops | bytes accessed | tf_op | source)
XLA Modules:
  0.0 417.0 jit_solution(2006850278856586799)
XLA Ops:
  0.0 6.1 %all-to-all-start = ((bf16[8,64,256]{2,1,0:T(8,128)(2,1)}), bf16[8,64,256]{2,1,0:T(8,128)(2,1)S(1)}, u32[]{:S(2)}, u32[]{:S(2)}) async-start(bf16[8,64,256]{2,1,0:T(8,128)(2,1)} %bitcast.90), calls=%async_computation | async-start | bytes 524288 | tf_op jit(solution)/shard_map/all_to_all | solution.py:45
  14.9 388.5 %while.15 = (s32[]{:T(128)}, f32[64,2048]{1,0:T(8,128)S(1)}, s32[]{:T(128)}, s32[32,10]{1,0:T(8,128)S(1)}, bf16[64,2048]{1,0:T(8,128)(2,1)S(1)}, /*index=5*/bf16...) while((s32[]{:T(128)}, f32[64,2048]{1,0:T(8,128)S(1)}, ...), condition=%wide.region_1.2_spmd, body=%wide.region_0.1_spmd.sunk | while | flops 39535096 | bytes 6292064 | solution.py:66
  14.9 5.6 %collective-permute-start = (f32[64,2048]{1,0:T(8,128)S(1)}, f32[64,2048]{1,0:T(8,128)S(1)}, u32[]{:S(2)}, u32[]{:S(2)}) collective-permute-start(f32[64,2048]{1,0:T(8,128)S(1)} %get-tuple-element.293), channel_id=1, source_target_pairs={{0,248},{8,0},{16,8},{24,16},{32,24},{40,32},{48,40},{56,48},{64,5... | collective-permute-start | bytes 1572872 | tf_op jit(solution)/shard_map/while/body/eval_jaxpr/ppermute | solution.py:9
  27.4 5.6 %collective-permute-start = (f32[64,2048]{1,0:T(8,128)S(1)}, f32[64,2048]{1,0:T(8,128)S(1)}, u32[]{:S(2)}, u32[]{:S(2)}) collective-permute-start(f32[64,2048]{1,0:T(8,128)S(1)} %get-tuple-element.293), channel_id=1, source_target_pairs={{0,248},{8,0},{16,8},{24,16},{32,24},{40,32},{48,40},{56,48},{64,5... | collective-permute-start | bytes 1572872 | tf_op jit(solution)/shard_map/while/body/eval_jaxpr/ppermute | solution.py:9
  39.9 5.6 %collective-permute-start = (f32[64,2048]{1,0:T(8,128)S(1)}, f32[64,2048]{1,0:T(8,128)S(1)}, u32[]{:S(2)}, u32[]{:S(2)}) collective-permute-start(f32[64,2048]{1,0:T(8,128)S(1)} %get-tuple-element.293), channel_id=1, source_target_pairs={{0,248},{8,0},{16,8},{24,16},{32,24},{40,32},{48,40},{56,48},{64,5... | collective-permute-start | bytes 1572872 | tf_op jit(solution)/shard_map/while/body/eval_jaxpr/ppermute | solution.py:9
  52.5 5.6 %collective-permute-start = (f32[64,2048]{1,0:T(8,128)S(1)}, f32[64,2048]{1,0:T(8,128)S(1)}, u32[]{:S(2)}, u32[]{:S(2)}) collective-permute-start(f32[64,2048]{1,0:T(8,128)S(1)} %get-tuple-element.293), channel_id=1, source_target_pairs={{0,248},{8,0},{16,8},{24,16},{32,24},{40,32},{48,40},{56,48},{64,5... | collective-permute-start | bytes 1572872 | tf_op jit(solution)/shard_map/while/body/eval_jaxpr/ppermute | solution.py:9
  65.0 5.6 %collective-permute-start = (f32[64,2048]{1,0:T(8,128)S(1)}, f32[64,2048]{1,0:T(8,128)S(1)}, u32[]{:S(2)}, u32[]{:S(2)}) collective-permute-start(f32[64,2048]{1,0:T(8,128)S(1)} %get-tuple-element.293), channel_id=1, source_target_pairs={{0,248},{8,0},{16,8},{24,16},{32,24},{40,32},{48,40},{56,48},{64,5... | collective-permute-start | bytes 1572872 | tf_op jit(solution)/shard_map/while/body/eval_jaxpr/ppermute | solution.py:9
  77.5 5.6 %collective-permute-start = (f32[64,2048]{1,0:T(8,128)S(1)}, f32[64,2048]{1,0:T(8,128)S(1)}, u32[]{:S(2)}, u32[]{:S(2)}) collective-permute-start(f32[64,2048]{1,0:T(8,128)S(1)} %get-tuple-element.293), channel_id=1, source_target_pairs={{0,248},{8,0},{16,8},{24,16},{32,24},{40,32},{48,40},{56,48},{64,5... | collective-permute-start | bytes 1572872 | tf_op jit(solution)/shard_map/while/body/eval_jaxpr/ppermute | solution.py:9
  90.0 5.6 %collective-permute-start = (f32[64,2048]{1,0:T(8,128)S(1)}, f32[64,2048]{1,0:T(8,128)S(1)}, u32[]{:S(2)}, u32[]{:S(2)}) collective-permute-start(f32[64,2048]{1,0:T(8,128)S(1)} %get-tuple-element.293), channel_id=1, source_target_pairs={{0,248},{8,0},{16,8},{24,16},{32,24},{40,32},{48,40},{56,48},{64,5... | collective-permute-start | bytes 1572872 | tf_op jit(solution)/shard_map/while/body/eval_jaxpr/ppermute | solution.py:9
  102.6 5.6 %collective-permute-start = (f32[64,2048]{1,0:T(8,128)S(1)}, f32[64,2048]{1,0:T(8,128)S(1)}, u32[]{:S(2)}, u32[]{:S(2)}) collective-permute-start(f32[64,2048]{1,0:T(8,128)S(1)} %get-tuple-element.293), channel_id=1, source_target_pairs={{0,248},{8,0},{16,8},{24,16},{32,24},{40,32},{48,40},{56,48},{64,5... | collective-permute-start | bytes 1572872 | tf_op jit(solution)/shard_map/while/body/eval_jaxpr/ppermute | solution.py:9
  115.1 5.6 %collective-permute-start = (f32[64,2048]{1,0:T(8,128)S(1)}, f32[64,2048]{1,0:T(8,128)S(1)}, u32[]{:S(2)}, u32[]{:S(2)}) collective-permute-start(f32[64,2048]{1,0:T(8,128)S(1)} %get-tuple-element.293), channel_id=1, source_target_pairs={{0,248},{8,0},{16,8},{24,16},{32,24},{40,32},{48,40},{56,48},{64,5... | collective-permute-start | bytes 1572872 | tf_op jit(solution)/shard_map/while/body/eval_jaxpr/ppermute | solution.py:9
  127.6 5.6 %collective-permute-start = (f32[64,2048]{1,0:T(8,128)S(1)}, f32[64,2048]{1,0:T(8,128)S(1)}, u32[]{:S(2)}, u32[]{:S(2)}) collective-permute-start(f32[64,2048]{1,0:T(8,128)S(1)} %get-tuple-element.293), channel_id=1, source_target_pairs={{0,248},{8,0},{16,8},{24,16},{32,24},{40,32},{48,40},{56,48},{64,5... | collective-permute-start | bytes 1572872 | tf_op jit(solution)/shard_map/while/body/eval_jaxpr/ppermute | solution.py:9
  140.1 5.6 %collective-permute-start = (f32[64,2048]{1,0:T(8,128)S(1)}, f32[64,2048]{1,0:T(8,128)S(1)}, u32[]{:S(2)}, u32[]{:S(2)}) collective-permute-start(f32[64,2048]{1,0:T(8,128)S(1)} %get-tuple-element.293), channel_id=1, source_target_pairs={{0,248},{8,0},{16,8},{24,16},{32,24},{40,32},{48,40},{56,48},{64,5... | collective-permute-start | bytes 1572872 | tf_op jit(solution)/shard_map/while/body/eval_jaxpr/ppermute | solution.py:9
  202.8 5.6 %collective-permute-start = (f32[64,2048]{1,0:T(8,128)S(1)}, f32[64,2048]{1,0:T(8,128)S(1)}, u32[]{:S(2)}, u32[]{:S(2)}) collective-permute-start(f32[64,2048]{1,0:T(8,128)S(1)} %get-tuple-element.293), channel_id=1, source_target_pairs={{0,248},{8,0},{16,8},{24,16},{32,24},{40,32},{48,40},{56,48},{64,5... | collective-permute-start | bytes 1572872 | tf_op jit(solution)/shard_map/while/body/eval_jaxpr/ppermute | solution.py:9
  227.8 5.6 %collective-permute-start = (f32[64,2048]{1,0:T(8,128)S(1)}, f32[64,2048]{1,0:T(8,128)S(1)}, u32[]{:S(2)}, u32[]{:S(2)}) collective-permute-start(f32[64,2048]{1,0:T(8,128)S(1)} %get-tuple-element.293), channel_id=1, source_target_pairs={{0,248},{8,0},{16,8},{24,16},{32,24},{40,32},{48,40},{56,48},{64,5... | collective-permute-start | bytes 1572872 | tf_op jit(solution)/shard_map/while/body/eval_jaxpr/ppermute | solution.py:9
  252.9 5.6 %collective-permute-start = (f32[64,2048]{1,0:T(8,128)S(1)}, f32[64,2048]{1,0:T(8,128)S(1)}, u32[]{:S(2)}, u32[]{:S(2)}) collective-permute-start(f32[64,2048]{1,0:T(8,128)S(1)} %get-tuple-element.293), channel_id=1, source_target_pairs={{0,248},{8,0},{16,8},{24,16},{32,24},{40,32},{48,40},{56,48},{64,5... | collective-permute-start | bytes 1572872 | tf_op jit(solution)/shard_map/while/body/eval_jaxpr/ppermute | solution.py:9
  277.9 5.6 %collective-permute-start = (f32[64,2048]{1,0:T(8,128)S(1)}, f32[64,2048]{1,0:T(8,128)S(1)}, u32[]{:S(2)}, u32[]{:S(2)}) collective-permute-start(f32[64,2048]{1,0:T(8,128)S(1)} %get-tuple-element.293), channel_id=1, source_target_pairs={{0,248},{8,0},{16,8},{24,16},{32,24},{40,32},{48,40},{56,48},{64,5... | collective-permute-start | bytes 1572872 | tf_op jit(solution)/shard_map/while/body/eval_jaxpr/ppermute | solution.py:9
  303.0 5.6 %collective-permute-start = (f32[64,2048]{1,0:T(8,128)S(1)}, f32[64,2048]{1,0:T(8,128)S(1)}, u32[]{:S(2)}, u32[]{:S(2)}) collective-permute-start(f32[64,2048]{1,0:T(8,128)S(1)} %get-tuple-element.293), channel_id=1, source_target_pairs={{0,248},{8,0},{16,8},{24,16},{32,24},{40,32},{48,40},{56,48},{64,5... | collective-permute-start | bytes 1572872 | tf_op jit(solution)/shard_map/while/body/eval_jaxpr/ppermute | solution.py:9
  328.0 5.6 %collective-permute-start = (f32[64,2048]{1,0:T(8,128)S(1)}, f32[64,2048]{1,0:T(8,128)S(1)}, u32[]{:S(2)}, u32[]{:S(2)}) collective-permute-start(f32[64,2048]{1,0:T(8,128)S(1)} %get-tuple-element.293), channel_id=1, source_target_pairs={{0,248},{8,0},{16,8},{24,16},{32,24},{40,32},{48,40},{56,48},{64,5... | collective-permute-start | bytes 1572872 | tf_op jit(solution)/shard_map/while/body/eval_jaxpr/ppermute | solution.py:9
  353.1 5.6 %collective-permute-start = (f32[64,2048]{1,0:T(8,128)S(1)}, f32[64,2048]{1,0:T(8,128)S(1)}, u32[]{:S(2)}, u32[]{:S(2)}) collective-permute-start(f32[64,2048]{1,0:T(8,128)S(1)} %get-tuple-element.293), channel_id=1, source_target_pairs={{0,248},{8,0},{16,8},{24,16},{32,24},{40,32},{48,40},{56,48},{64,5... | collective-permute-start | bytes 1572872 | tf_op jit(solution)/shard_map/while/body/eval_jaxpr/ppermute | solution.py:9
  378.1 5.6 %collective-permute-start = (f32[64,2048]{1,0:T(8,128)S(1)}, f32[64,2048]{1,0:T(8,128)S(1)}, u32[]{:S(2)}, u32[]{:S(2)}) collective-permute-start(f32[64,2048]{1,0:T(8,128)S(1)} %get-tuple-element.293), channel_id=1, source_target_pairs={{0,248},{8,0},{16,8},{24,16},{32,24},{40,32},{48,40},{56,48},{64,5... | collective-permute-start | bytes 1572872 | tf_op jit(solution)/shard_map/while/body/eval_jaxpr/ppermute | solution.py:9
  390.6 5.7 %collective-permute-start = (f32[64,2048]{1,0:T(8,128)S(1)}, f32[64,2048]{1,0:T(8,128)S(1)}, u32[]{:S(2)}, u32[]{:S(2)}) collective-permute-start(f32[64,2048]{1,0:T(8,128)S(1)} %get-tuple-element.293), channel_id=1, source_target_pairs={{0,248},{8,0},{16,8},{24,16},{32,24},{40,32},{48,40},{56,48},{64,5... | collective-permute-start | bytes 1572872 | tf_op jit(solution)/shard_map/while/body/eval_jaxpr/ppermute | solution.py:9
  404.1 5.7 %all-to-all-start.1 = ((bf16[64,8,256]{2,0,1:T(8,128)(2,1)}), bf16[64,8,256]{2,0,1:T(8,128)(2,1)S(1)}, u32[]{:S(2)}, u32[]{:S(2)}) async-start(bf16[64,8,256]{2,0,1:T(8,128)(2,1)} %bitcast.61), calls=%async_computation.1 | async-start | bytes 524288 | tf_op jit(solution)/shard_map/all_to_all | solution.py:68
  410.1 5.8 %all-to-all-done.1 = bf16[64,8,256]{2,0,1:T(8,128)(2,1)S(1)} async-done(((bf16[64,8,256]{2,0,1:T(8,128)(2,1)}), bf16[64,8,256]{2,0,1:T(8,128)(2,1)S(1)}, u32[]{:S(2)}, u32[]{:S(2)}) %all-to-all-start.1) | async-done | bytes 262176 | tf_op jit(solution)/shard_map/all_to_all | solution.py:68
  (316 shorter events, 286.0 us)
Async XLA Ops:
  14.9 12.3 %collective-permute-start = (f32[64,2048]{1,0:T(8,128)S(1)}, f32[64,2048]{1,0:T(8,128)S(1)}, u32[]{:S(2)}, u32[]{:S(2)}) collective-permute-start(f32[64,2048]{1,0:T(8,128)S(1)} %get-tuple-element.293), channel_id=1, source_target_pairs={{0,248},{8,0},{16,8},{24,16},{32,24},{40,32},{48,40},{56,48},{64,5... | collective-permute-start | bytes 1572872 | tf_op jit(solution)/shard_map/while/body/eval_jaxpr/ppermute | solution.py:9
  27.4 12.3 %collective-permute-start = (f32[64,2048]{1,0:T(8,128)S(1)}, f32[64,2048]{1,0:T(8,128)S(1)}, u32[]{:S(2)}, u32[]{:S(2)}) collective-permute-start(f32[64,2048]{1,0:T(8,128)S(1)} %get-tuple-element.293), channel_id=1, source_target_pairs={{0,248},{8,0},{16,8},{24,16},{32,24},{40,32},{48,40},{56,48},{64,5... | collective-permute-start | bytes 1572872 | tf_op jit(solution)/shard_map/while/body/eval_jaxpr/ppermute | solution.py:9
  39.9 12.3 %collective-permute-start = (f32[64,2048]{1,0:T(8,128)S(1)}, f32[64,2048]{1,0:T(8,128)S(1)}, u32[]{:S(2)}, u32[]{:S(2)}) collective-permute-start(f32[64,2048]{1,0:T(8,128)S(1)} %get-tuple-element.293), channel_id=1, source_target_pairs={{0,248},{8,0},{16,8},{24,16},{32,24},{40,32},{48,40},{56,48},{64,5... | collective-permute-start | bytes 1572872 | tf_op jit(solution)/shard_map/while/body/eval_jaxpr/ppermute | solution.py:9
  52.5 12.3 %collective-permute-start = (f32[64,2048]{1,0:T(8,128)S(1)}, f32[64,2048]{1,0:T(8,128)S(1)}, u32[]{:S(2)}, u32[]{:S(2)}) collective-permute-start(f32[64,2048]{1,0:T(8,128)S(1)} %get-tuple-element.293), channel_id=1, source_target_pairs={{0,248},{8,0},{16,8},{24,16},{32,24},{40,32},{48,40},{56,48},{64,5... | collective-permute-start | bytes 1572872 | tf_op jit(solution)/shard_map/while/body/eval_jaxpr/ppermute | solution.py:9
  65.0 12.3 %collective-permute-start = (f32[64,2048]{1,0:T(8,128)S(1)}, f32[64,2048]{1,0:T(8,128)S(1)}, u32[]{:S(2)}, u32[]{:S(2)}) collective-permute-start(f32[64,2048]{1,0:T(8,128)S(1)} %get-tuple-element.293), channel_id=1, source_target_pairs={{0,248},{8,0},{16,8},{24,16},{32,24},{40,32},{48,40},{56,48},{64,5... | collective-permute-start | bytes 1572872 | tf_op jit(solution)/shard_map/while/body/eval_jaxpr/ppermute | solution.py:9
  77.5 12.3 %collective-permute-start = (f32[64,2048]{1,0:T(8,128)S(1)}, f32[64,2048]{1,0:T(8,128)S(1)}, u32[]{:S(2)}, u32[]{:S(2)}) collective-permute-start(f32[64,2048]{1,0:T(8,128)S(1)} %get-tuple-element.293), channel_id=1, source_target_pairs={{0,248},{8,0},{16,8},{24,16},{32,24},{40,32},{48,40},{56,48},{64,5... | collective-permute-start | bytes 1572872 | tf_op jit(solution)/shard_map/while/body/eval_jaxpr/ppermute | solution.py:9
  90.0 12.3 %collective-permute-start = (f32[64,2048]{1,0:T(8,128)S(1)}, f32[64,2048]{1,0:T(8,128)S(1)}, u32[]{:S(2)}, u32[]{:S(2)}) collective-permute-start(f32[64,2048]{1,0:T(8,128)S(1)} %get-tuple-element.293), channel_id=1, source_target_pairs={{0,248},{8,0},{16,8},{24,16},{32,24},{40,32},{48,40},{56,48},{64,5... | collective-permute-start | bytes 1572872 | tf_op jit(solution)/shard_map/while/body/eval_jaxpr/ppermute | solution.py:9
  102.6 12.3 %collective-permute-start = (f32[64,2048]{1,0:T(8,128)S(1)}, f32[64,2048]{1,0:T(8,128)S(1)}, u32[]{:S(2)}, u32[]{:S(2)}) collective-permute-start(f32[64,2048]{1,0:T(8,128)S(1)} %get-tuple-element.293), channel_id=1, source_target_pairs={{0,248},{8,0},{16,8},{24,16},{32,24},{40,32},{48,40},{56,48},{64,5... | collective-permute-start | bytes 1572872 | tf_op jit(solution)/shard_map/while/body/eval_jaxpr/ppermute | solution.py:9
  115.1 12.3 %collective-permute-start = (f32[64,2048]{1,0:T(8,128)S(1)}, f32[64,2048]{1,0:T(8,128)S(1)}, u32[]{:S(2)}, u32[]{:S(2)}) collective-permute-start(f32[64,2048]{1,0:T(8,128)S(1)} %get-tuple-element.293), channel_id=1, source_target_pairs={{0,248},{8,0},{16,8},{24,16},{32,24},{40,32},{48,40},{56,48},{64,5... | collective-permute-start | bytes 1572872 | tf_op jit(solution)/shard_map/while/body/eval_jaxpr/ppermute | solution.py:9
  127.6 12.3 %collective-permute-start = (f32[64,2048]{1,0:T(8,128)S(1)}, f32[64,2048]{1,0:T(8,128)S(1)}, u32[]{:S(2)}, u32[]{:S(2)}) collective-permute-start(f32[64,2048]{1,0:T(8,128)S(1)} %get-tuple-element.293), channel_id=1, source_target_pairs={{0,248},{8,0},{16,8},{24,16},{32,24},{40,32},{48,40},{56,48},{64,5... | collective-permute-start | bytes 1572872 | tf_op jit(solution)/shard_map/while/body/eval_jaxpr/ppermute | solution.py:9
  140.1 12.3 %collective-permute-start = (f32[64,2048]{1,0:T(8,128)S(1)}, f32[64,2048]{1,0:T(8,128)S(1)}, u32[]{:S(2)}, u32[]{:S(2)}) collective-permute-start(f32[64,2048]{1,0:T(8,128)S(1)} %get-tuple-element.293), channel_id=1, source_target_pairs={{0,248},{8,0},{16,8},{24,16},{32,24},{40,32},{48,40},{56,48},{64,5... | collective-permute-start | bytes 1572872 | tf_op jit(solution)/shard_map/while/body/eval_jaxpr/ppermute | solution.py:9
  152.7 12.3 %collective-permute-start = (f32[64,2048]{1,0:T(8,128)S(1)}, f32[64,2048]{1,0:T(8,128)S(1)}, u32[]{:S(2)}, u32[]{:S(2)}) collective-permute-start(f32[64,2048]{1,0:T(8,128)S(1)} %get-tuple-element.293), channel_id=1, source_target_pairs={{0,248},{8,0},{16,8},{24,16},{32,24},{40,32},{48,40},{56,48},{64,5... | collective-permute-start | bytes 1572872 | tf_op jit(solution)/shard_map/while/body/eval_jaxpr/ppermute | solution.py:9
  165.2 12.3 %collective-permute-start = (f32[64,2048]{1,0:T(8,128)S(1)}, f32[64,2048]{1,0:T(8,128)S(1)}, u32[]{:S(2)}, u32[]{:S(2)}) collective-permute-start(f32[64,2048]{1,0:T(8,128)S(1)} %get-tuple-element.293), channel_id=1, source_target_pairs={{0,248},{8,0},{16,8},{24,16},{32,24},{40,32},{48,40},{56,48},{64,5... | collective-permute-start | bytes 1572872 | tf_op jit(solution)/shard_map/while/body/eval_jaxpr/ppermute | solution.py:9
  177.7 12.3 %collective-permute-start = (f32[64,2048]{1,0:T(8,128)S(1)}, f32[64,2048]{1,0:T(8,128)S(1)}, u32[]{:S(2)}, u32[]{:S(2)}) collective-permute-start(f32[64,2048]{1,0:T(8,128)S(1)} %get-tuple-element.293), channel_id=1, source_target_pairs={{0,248},{8,0},{16,8},{24,16},{32,24},{40,32},{48,40},{56,48},{64,5... | collective-permute-start | bytes 1572872 | tf_op jit(solution)/shard_map/while/body/eval_jaxpr/ppermute | solution.py:9
  190.2 12.3 %collective-permute-start = (f32[64,2048]{1,0:T(8,128)S(1)}, f32[64,2048]{1,0:T(8,128)S(1)}, u32[]{:S(2)}, u32[]{:S(2)}) collective-permute-start(f32[64,2048]{1,0:T(8,128)S(1)} %get-tuple-element.293), channel_id=1, source_target_pairs={{0,248},{8,0},{16,8},{24,16},{32,24},{40,32},{48,40},{56,48},{64,5... | collective-permute-start | bytes 1572872 | tf_op jit(solution)/shard_map/while/body/eval_jaxpr/ppermute | solution.py:9
  202.8 12.3 %collective-permute-start = (f32[64,2048]{1,0:T(8,128)S(1)}, f32[64,2048]{1,0:T(8,128)S(1)}, u32[]{:S(2)}, u32[]{:S(2)}) collective-permute-start(f32[64,2048]{1,0:T(8,128)S(1)} %get-tuple-element.293), channel_id=1, source_target_pairs={{0,248},{8,0},{16,8},{24,16},{32,24},{40,32},{48,40},{56,48},{64,5... | collective-permute-start | bytes 1572872 | tf_op jit(solution)/shard_map/while/body/eval_jaxpr/ppermute | solution.py:9
  227.8 12.3 %collective-permute-start = (f32[64,2048]{1,0:T(8,128)S(1)}, f32[64,2048]{1,0:T(8,128)S(1)}, u32[]{:S(2)}, u32[]{:S(2)}) collective-permute-start(f32[64,2048]{1,0:T(8,128)S(1)} %get-tuple-element.293), channel_id=1, source_target_pairs={{0,248},{8,0},{16,8},{24,16},{32,24},{40,32},{48,40},{56,48},{64,5... | collective-permute-start | bytes 1572872 | tf_op jit(solution)/shard_map/while/body/eval_jaxpr/ppermute | solution.py:9
  252.9 12.3 %collective-permute-start = (f32[64,2048]{1,0:T(8,128)S(1)}, f32[64,2048]{1,0:T(8,128)S(1)}, u32[]{:S(2)}, u32[]{:S(2)}) collective-permute-start(f32[64,2048]{1,0:T(8,128)S(1)} %get-tuple-element.293), channel_id=1, source_target_pairs={{0,248},{8,0},{16,8},{24,16},{32,24},{40,32},{48,40},{56,48},{64,5... | collective-permute-start | bytes 1572872 | tf_op jit(solution)/shard_map/while/body/eval_jaxpr/ppermute | solution.py:9
  277.9 12.3 %collective-permute-start = (f32[64,2048]{1,0:T(8,128)S(1)}, f32[64,2048]{1,0:T(8,128)S(1)}, u32[]{:S(2)}, u32[]{:S(2)}) collective-permute-start(f32[64,2048]{1,0:T(8,128)S(1)} %get-tuple-element.293), channel_id=1, source_target_pairs={{0,248},{8,0},{16,8},{24,16},{32,24},{40,32},{48,40},{56,48},{64,5... | collective-permute-start | bytes 1572872 | tf_op jit(solution)/shard_map/while/body/eval_jaxpr/ppermute | solution.py:9
  303.0 12.3 %collective-permute-start = (f32[64,2048]{1,0:T(8,128)S(1)}, f32[64,2048]{1,0:T(8,128)S(1)}, u32[]{:S(2)}, u32[]{:S(2)}) collective-permute-start(f32[64,2048]{1,0:T(8,128)S(1)} %get-tuple-element.293), channel_id=1, source_target_pairs={{0,248},{8,0},{16,8},{24,16},{32,24},{40,32},{48,40},{56,48},{64,5... | collective-permute-start | bytes 1572872 | tf_op jit(solution)/shard_map/while/body/eval_jaxpr/ppermute | solution.py:9
  328.0 12.3 %collective-permute-start = (f32[64,2048]{1,0:T(8,128)S(1)}, f32[64,2048]{1,0:T(8,128)S(1)}, u32[]{:S(2)}, u32[]{:S(2)}) collective-permute-start(f32[64,2048]{1,0:T(8,128)S(1)} %get-tuple-element.293), channel_id=1, source_target_pairs={{0,248},{8,0},{16,8},{24,16},{32,24},{40,32},{48,40},{56,48},{64,5... | collective-permute-start | bytes 1572872 | tf_op jit(solution)/shard_map/while/body/eval_jaxpr/ppermute | solution.py:9
  353.1 12.3 %collective-permute-start = (f32[64,2048]{1,0:T(8,128)S(1)}, f32[64,2048]{1,0:T(8,128)S(1)}, u32[]{:S(2)}, u32[]{:S(2)}) collective-permute-start(f32[64,2048]{1,0:T(8,128)S(1)} %get-tuple-element.293), channel_id=1, source_target_pairs={{0,248},{8,0},{16,8},{24,16},{32,24},{40,32},{48,40},{56,48},{64,5... | collective-permute-start | bytes 1572872 | tf_op jit(solution)/shard_map/while/body/eval_jaxpr/ppermute | solution.py:9
  378.1 12.3 %collective-permute-start = (f32[64,2048]{1,0:T(8,128)S(1)}, f32[64,2048]{1,0:T(8,128)S(1)}, u32[]{:S(2)}, u32[]{:S(2)}) collective-permute-start(f32[64,2048]{1,0:T(8,128)S(1)} %get-tuple-element.293), channel_id=1, source_target_pairs={{0,248},{8,0},{16,8},{24,16},{32,24},{40,32},{48,40},{56,48},{64,5... | collective-permute-start | bytes 1572872 | tf_op jit(solution)/shard_map/while/body/eval_jaxpr/ppermute | solution.py:9
  390.6 12.4 %collective-permute-start = (f32[64,2048]{1,0:T(8,128)S(1)}, f32[64,2048]{1,0:T(8,128)S(1)}, u32[]{:S(2)}, u32[]{:S(2)}) collective-permute-start(f32[64,2048]{1,0:T(8,128)S(1)} %get-tuple-element.293), channel_id=1, source_target_pairs={{0,248},{8,0},{16,8},{24,16},{32,24},{40,32},{48,40},{56,48},{64,5... | collective-permute-start | bytes 1572872 | tf_op jit(solution)/shard_map/while/body/eval_jaxpr/ppermute | solution.py:9
  (12 other events, 1315.8 us)
where the time goes:
time: 419 us; the launch traced here: 417 us
  starting transfers between devices  185 us (44%)
  waiting for transfers between devices  86.1 us (21%)
  matrix products  70.7 us (17%)
  local copies, waits for them, and re-layouts  45.3 us (11%)
  other arithmetic  28.2 us (7%)
    ppermute x31, starting transfers between devices, from_behind(): lax.ppermute(shard, axis, [(i, (i + by) % size) for i in range(size)])  174 us
    ppermute x31, waiting for transfers between devices, from_behind(): lax.ppermute(shard, axis, [(i, (i + by) % size) for i in range(size)])  79.5 us
    dot_general x32, matrix products, tile_terms(): jnp.einsum('kfc,krc->kfr', chosen, tiles, preferred_element_type=jnp.floa...  41.2 us
    dynamic_slice x32, local copies, waits for them, and re-layouts, contribution(): lax.dynamic_index_in_dim(own_counts, target, 0, False)  40 us
    lt x32, other arithmetic, tile_terms(): active = lax.iota(jnp.int32, slot_count) < filled  20 us
    dot_general x32, matrix products, tile_terms(): jnp.einsum('kb,kfr->fbr', placer, products, precision=lax.Precision.HIGHE...  19.9 us
    dot_general x32, matrix products, tile_terms(): jnp.einsum('kb,fbc->kfc', picker, grouped, preferred_element_type=jnp.flo...  8.9 us
  transfers between devices with their start and end apart: 33, of which 33 were waited for; matrix products, arithmetic and copies ran while one was open for 32% of the time, Pallas kernels for 0%

commit v1 on v0

v1 whole, which is shorter than its diff:
```python
import jax
import jax.numpy as jnp
from jax import lax
from jax.experimental import pallas as pl
from jax.experimental.pallas import tpu as pltpu
from jax.sharding import Mesh
from jax.sharding import PartitionSpec as P

RINGS = 8
SIDES = 2
CORES = 2
VMEM = 10 * 1024 * 1024


def tile_kernel(targets, codes, columns, tiles, *rest):
    partner, out = rest if len(rest) == 2 else (None, rest[0])
    blocks, channels, edge = out.shape[1:]
    slots = tiles.shape[1]
    target = targets[pl.program_id(0)]
    acc = out.at[0]
    acc[...] = jnp.zeros_like(acc) if partner is None else partner[0]
    per = columns.shape[2] // edge
    for slot in range(slots):
        code = codes[target * slots + slot]
        row, col = code // blocks, code % blocks
        lanes = pl.ds(pl.multiple_of((col % per) * edge, edge), edge)

        @pl.when(row < blocks)
        def _():
            chosen = columns[col // per, :, lanes]
            acc[row] += lax.dot_general(
                chosen, tiles[0, slot], (((1,), (1,)), ((), ())), preferred_element_type=jnp.float32
            )


def tile_sums(targets, codes, columns, tiles, partner=None):
    count = targets.shape[0]
    slots, edge = tiles.shape[1], tiles.shape[2]
    channels = columns.shape[1]
    blocks = columns.shape[0] * columns.shape[2] // edge
    dense = pl.BlockSpec((1, blocks, channels, edge), lambda i, *_: (i, 0, 0, 0))
    in_specs = [
        pl.BlockSpec(columns.shape, lambda i, *_: (0, 0, 0)),
        pl.BlockSpec((1, slots, edge, edge), lambda i, t, c: (t[i], 0, 0, 0)),
    ]
    operands = [columns, tiles]
    if partner is not None:
        in_specs.append(dense)
        operands.append(partner)
    return pl.pallas_call(
        tile_kernel,
        grid_spec=pltpu.PrefetchScalarGridSpec(
            num_scalar_prefetch=2, grid=(count,), in_specs=in_specs, out_specs=dense
        ),
        out_shape=jax.ShapeDtypeStruct((count, blocks, channels, edge), jnp.float32),
        compiler_params=pltpu.CompilerParams(vmem_limit_bytes=VMEM),
        cost_estimate=pl.CostEstimate(
            flops=count * 1_500_000_000, bytes_accessed=count * 800_000, transcendentals=0
        ),
    )(targets, codes, *operands)


def finish_kernel(base, neighbors, weight, out):
    size = neighbors.shape[0] * neighbors.shape[2]
    edge = neighbors.shape[3]
    for half in range(neighbors.shape[1]):
        features = neighbors[:, half].reshape(size, edge)
        lanes = slice(half * edge, (half + 1) * edge)
        combined = base[:, lanes] + lax.dot_general(
            weight[...], features, (((0,), (0,)), ((), ())), preferred_element_type=jnp.float32
        )
        hidden = jnp.maximum(combined, 0.0)
        mean_square = jnp.mean(hidden * hidden, axis=0, keepdims=True)
        out[:, lanes] = (hidden * lax.rsqrt(mean_square + 1e-05)).astype(out.dtype)


def finish(base, neighbors, weight):
    return pl.pallas_call(
        finish_kernel,
        out_shape=jax.ShapeDtypeStruct(base.shape, jnp.bfloat16),
        compiler_params=pltpu.CompilerParams(vmem_limit_bytes=VMEM),
    )(base, neighbors, weight)


def hop(values, by):
    return lax.ppermute(values, "ring", [(i, (i + by) % RINGS) for i in range(RINGS)])


def swap(values, axis):
    return lax.ppermute(values, axis, [(0, 1), (1, 0)])


def shards(node_feats, tile_vals, tile_rows, tile_cols, tile_count, degree, w_self, w_neigh):
    groups = lax.axis_size("grp")
    features, width = node_feats.shape
    ring = lax.axis_index("ring")
    side = lax.axis_index("side")
    core = lax.axis_index("core")
    columns = lax.all_to_all(
        node_feats.reshape(groups, features // groups, width), "grp", split_axis=0, concat_axis=0
    )
    tiles = tile_vals[0]
    targets_count, slots, edge = tiles.shape[:3]
    blocks = groups * width // edge
    active = lax.broadcasted_iota(jnp.int32, (targets_count, slots), 1) < tile_count[0][:, None]
    codes = (jnp.where(active, tile_rows[0], blocks) * blocks + tile_cols[0]).reshape(-1)

    def indices(steps, core_index):
        position = [((ring + by + RINGS) % RINGS * SIDES + side_index) * CORES + core_index for by, side_index in steps]
        return jnp.stack(position).astype(jnp.int32)

    mine, other = side, 1 - side
    plan = [
        [(4, mine), (-4, other)],
        [(3, mine), (3, other), (-3, mine), (-3, other)],
        [(2, mine), (2, other), (-2, mine), (-2, other)],
        [(1, mine), (1, other), (-1, mine), (-1, other)],
        [(0, mine), (0, other)],
    ]
    local = []
    for steps in plan:
        foreign = tile_sums(indices(steps, 1 - core), codes, columns, tiles)
        partner = swap(foreign, "core")
        local.append(tile_sums(indices(steps, core), codes, columns, tiles, partner))

    def low(values):
        return values.astype(jnp.bfloat16)

    up = hop(low(local[0][:1]), 1).astype(jnp.float32)
    down = hop(low(local[0][1:]), -1).astype(jnp.float32)
    here = local[1]
    send_up = jnp.stack([low(here[0] + up[0]), low(here[1])])
    send_down = jnp.stack([low(here[2]), low(here[3] + down[0])])
    for here in local[2:4]:
        up = hop(send_up, 1).astype(jnp.float32)
        down = hop(send_down, -1).astype(jnp.float32)
        send_up = low(here[:2] + up)
        send_down = low(here[2:] + down)
    up = hop(send_up, 1).astype(jnp.float32)
    down = hop(send_down, -1).astype(jnp.float32)
    own = local[4] + up + down
    summed = own[0] + swap(low(own[1]), "side").astype(jnp.float32)
    neighbor = low(summed / degree.astype(jnp.float32).reshape(blocks, 1, edge))
    neighbor = neighbor.reshape(groups, blocks // groups, features // groups, edge)
    gathered = lax.all_to_all(neighbor, "grp", split_axis=0, concat_axis=0)
    base = lax.dot_general(
        w_self, node_feats, (((0,), (0,)), ((), ())), preferred_element_type=jnp.float32
    )
    return finish(base, gathered, w_neigh)


def solution(mesh):
    fine = Mesh(
        mesh.devices.reshape(RINGS, SIDES, CORES, mesh.shape["grp"]), ("ring", "side", "core", "grp")
    )
    loop = ("ring", "side", "core")
    return jax.shard_map(
        shards,
        mesh=fine,
        in_specs=(
            P(None, (*loop, "grp")),
            P(loop, None, None, None, None),
            P(loop, None, None),
            P(loop, None, None),
            P(loop, None),
            P(loop),
            P(),
            P(),
        ),
        out_specs=P(None, (*loop, "grp")),
        check_vma=False,
    )
```

time: 419 us -> 126 us (0.30)
  starting transfers between devices: 185 us -> 33.6 us
  matrix products: 70.7 us -> 0.34 us
  waiting for transfers between devices: 86.1 us -> 34.2 us
  Pallas kernels: 0 us -> 40.6 us
  local copies, waits for them, and re-layouts: 45.3 us -> 10 us
  other arithmetic: 28.2 us -> 5.79 us
    ppermute x31 -> x14, starting transfers between devices: 174 us -> 22.4 us  [the longest x8 12.2 us: hop(): lax.ppermute(values, 'ring', [(i, (i + by) % RINGS) for i in range(RINGS)])]
    dot_general x98 -> x1, matrix products: 70.7 us -> 0.34 us  [shards(): lax.dot_general(w_self, node_feats, (((0,), (0,)), ((), ())), preferred_e...]
    ppermute x31 -> x14, waiting for transfers between devices: 79.5 us -> 25.6 us  [the longest x8 21.2 us: hop(): lax.ppermute(values, 'ring', [(i, (i + by) % RINGS) for i in range(RINGS)])]
    dynamic_slice x33 -> x0, local copies, waits for them, and re-layouts: 41.3 us -> none  [the longest x32 40 us: contribution(): lax.dynamic_index_in_dim(own_counts, target, 0, False)]
    pallas_call x0 -> x11, Pallas kernels: none -> 40.6 us  [the longest x10 39.3 us: tile_sums(): pl.pallas_call(tile_kernel, grid_spec=pltpu.PrefetchScalarGridSpec(num_sc...]
    lt x32 -> x1, other arithmetic: 20 us -> 0.73 us  [shards(): lax.broadcasted_iota(jnp.int32, (targets_count, slots), 1)]
    unnamed x9 -> x20, local copies, waits for them, and re-layouts: 1.71 us -> 9.59 us
    add x31 -> x2, other arithmetic: 6.66 us -> 1.28 us  [the longest x1 1.28 us: shards(): own = local[4] + up + down]
  transfers between devices with their start and end apart: 33 -> 16, of which waited for: 33 -> 10; matrix products, arithmetic and copies ran while one was open for 32% -> 5% of each run, Pallas kernels for 0% -> 28%
where the time goes in v1:
time: 126 us; the launch traced here: 125 us
  Pallas kernels  40.6 us (32%)
  waiting for transfers between devices  34.2 us (27%)
  starting transfers between devices  33.6 us (27%)
  local copies, waits for them, and re-layouts  10 us (8%)
  other arithmetic  5.79 us (5%)
    pallas_call x10, Pallas kernels, tile_sums(): pl.pallas_call(tile_kernel, grid_spec=pltpu.PrefetchScalarGridSpec(num_sc...  39.3 us
    ppermute x8, waiting for transfers between devices, hop(): lax.ppermute(values, 'ring', [(i, (i + by) % RINGS) for i in range(RINGS)])  21.2 us
    ppermute x8, starting transfers between devices, hop(): lax.ppermute(values, 'ring', [(i, (i + by) % RINGS) for i in range(RINGS)])  12.2 us
    ppermute x6, starting transfers between devices, swap(): return lax.ppermute(values, axis, [(0, 1), (1, 0)])  10.2 us
    unnamed x20, local copies, waits for them, and re-layouts  9.59 us
    all_to_all x1, starting transfers between devices, shards(): lax.all_to_all(node_feats.reshape(groups, features // groups, width), 'gr...  6.06 us
    all_to_all x1, waiting for transfers between devices, shards(): gathered = lax.all_to_all(neighbor, 'grp', split_axis=0, concat_axis=0)  5.79 us
    all_to_all x1, starting transfers between devices, shards(): gathered = lax.all_to_all(neighbor, 'grp', split_axis=0, concat_axis=0)  5.09 us
  transfers between devices with their start and end apart: 16, of which 10 were waited for; matrix products, arithmetic and copies ran while one was open for 5% of the time, Pallas kernels for 28%

profile of v1, /device:TPU:2, one launch (start us, length us, event | category | flops | bytes accessed | tf_op | source)
XLA Modules:
  0.0 124.7 jit_solution(5124425465784342605)
XLA Ops:
  0.0 6.1 %all-to-all-start = ((bf16[8,64,256]{2,1,0:T(8,128)(2,1)}), bf16[8,64,256]{2,1,0:T(8,128)(2,1)S(1)}, u32[]{:S(2)}, u32[]{:S(2)}) async-start(bf16[8,64,256]{2,1,0:T(8,128)(2,1)} %bitcast.62), calls=%async_computation | async-start | bytes 524288 | tf_op jit(solution)/shard_map/all_to_all | solution.py:99
  9.4 2.8 %all-to-all-done.columns = bf16[8,64,256]{2,1,0:T(8,128)(2,1)S(1)} async-done(((bf16[8,64,256]{2,1,0:T(8,128)(2,1)}), bf16[8,64,256]{2,1,0:T(8,128)(2,1)S(1)}, u32[]{:S(2)}, u32[]{:S(2)}) %all-to-all-start) | async-done | bytes 262176 | tf_op jit(solution)/shard_map/all_to_all | solution.py:99
  12.2 4.0 %copy-done.1 = bf16[1,32,10,128,128]{4,3,2,1,0:T(8,128)(2,1)S(1)} copy-done((bf16[1,32,10,128,128]{4,3,2,1,0:T(8,128)(2,1)S(1)}, bf16[1,32,10,128,128]{4,3,2,1,0:T(8,128)(2,1)}, u32[]{:S(2)}) %copy-start.1) | copy-done | bytes 10485784
  16.2 4.7 %shard_map.88 = f32[4,16,64,128]{3,2,1,0:T(8,128)S(1)} custom-call(s32[4]{0:T(128)S(1)} %pad_add_fusion.7.targets, s32[320]{0:T(512)S(1)} %multiply_add_fusion.codes, bf16[8,64,256]{2,1,0:T(8,128)(2,1)S(1)} %all-to-all-done.columns, bf16[32,10,128,128]{3,2,1,0:T(8,128)(2,1)S(1)} %bitcast.50), custom_call_target="tpu_custom_call" | custom-call | flops 6000000000 | bytes 3200000 | tf_op jit(solution)/shard_map/pallas_call | solution.py:50
  21.0 2.2 %shard_map.90 = f32[2,16,64,128]{3,2,1,0:T(8,128)S(1)} custom-call(s32[2]{0:T(128)S(1)} %pad_add_fusion.9.targets, s32[320]{0:T(512)S(1)} %multiply_add_fusion.codes, bf16[8,64,256]{2,1,0:T(8,128)(2,1)S(1)} %all-to-all-done.columns, bf16[32,10,128,128]{3,2,1,0:T(8,128)(2,1)S(1)} %bitcast.51), custom_call_target="tpu_custom_call" | custom-call | flops 3000000000 | bytes 1600000 | tf_op jit(solution)/shard_map/pallas_call | solution.py:50
  24.4 5.0 %shard_map.86 = f32[4,16,64,128]{3,2,1,0:T(8,128)S(1)} custom-call(s32[4]{0:T(128)S(1)} %pad_add_fusion.5.targets, s32[320]{0:T(512)S(1)} %multiply_add_fusion.codes, bf16[8,64,256]{2,1,0:T(8,128)(2,1)S(1)} %all-to-all-done.columns, bf16[32,10,128,128]{3,2,1,0:T(8,128)(2,1)S(1)} %bitcast.52), custom_call_target="tpu_custom_call" | custom-call | flops 6000000000 | bytes 3200000 | tf_op jit(solution)/shard_map/pallas_call | solution.py:50
  29.7 4.4 %shard_map.84 = f32[4,16,64,128]{3,2,1,0:T(8,128)S(1)} custom-call(s32[4]{0:T(128)S(1)} %pad_add_fusion.3.targets, s32[320]{0:T(512)S(1)} %multiply_add_fusion.codes, bf16[8,64,256]{2,1,0:T(8,128)(2,1)S(1)} %all-to-all-done.columns, bf16[32,10,128,128]{3,2,1,0:T(8,128)(2,1)S(1)} %bitcast.55), custom_call_target="tpu_custom_call" | custom-call | flops 6000000000 | bytes 3200000 | tf_op jit(solution)/shard_map/pallas_call | solution.py:50
  36.0 3.1 %shard_map.82 = f32[2,16,64,128]{3,2,1,0:T(8,128)S(1)} custom-call(s32[2]{0:T(128)S(1)} %pad_add_fusion.1.targets, s32[320]{0:T(512)S(1)} %multiply_add_fusion.codes, bf16[8,64,256]{2,1,0:T(8,128)(2,1)S(1)} %all-to-all-done.columns, bf16[32,10,128,128]{3,2,1,0:T(8,128)(2,1)S(1)} %bitcast.56), custom_call_target="tpu_custom_call" | custom-call | flops 3000000000 | bytes 1600000 | tf_op jit(solution)/shard_map/pallas_call | solution.py:50
  39.4 2.1 %shard_map.91 = f32[2,16,64,128]{3,2,1,0:T(8,128)S(1)} custom-call(s32[2]{0:T(128)S(1)} %pad_add_fusion.8.targets, s32[320]{0:T(512)S(1)} %multiply_add_fusion.codes, bf16[8,64,256]{2,1,0:T(8,128)(2,1)S(1)} %all-to-all-done.columns, bf16[32,10,128,128]{3,2,1,0:T(8,128)(2,1)S(1)} %bitcast.57, f32[2,16,64,128]{3,2,1,0:T(8,128)S(1)} %collective-permute-done.4.rest_0_), custom_call_target="tpu_custom_call" | custom-call | flops 3000000000 | bytes 1600000 | tf_op jit(solution)/shard_map/pallas_call | solution.py:50
  41.8 4.8 %collective-permute-start.9 = (bf16[1,16,64,128]{3,2,1,0:T(8,128)(2,1)S(1)}, bf16[1,16,64,128]{3,2,1,0:T(8,128)(2,1)S(1)}, u32[]{:S(2)}, u32[]{:S(2)}) collective-permute-start(bf16[1,16,64,128]{3,2,1,0:T(8,128)(2,1)S(1)} %get-tuple-element.14), channel_id=1, source_target_pairs={{0,224},{32,0},{64,32},{96,64},{128,96},{160,128},{192,160},{224,1... | collective-permute-start | bytes 786440 | tf_op jit(solution)/shard_map/ppermute | solution.py:86
  46.6 4.5 %shard_map.89 = f32[4,16,64,128]{3,2,1,0:T(8,128)S(1)} custom-call(s32[4]{0:T(128)S(1)} %pad_add_fusion.6.targets, s32[320]{0:T(512)S(1)} %multiply_add_fusion.codes, bf16[8,64,256]{2,1,0:T(8,128)(2,1)S(1)} %all-to-all-done.columns, bf16[32,10,128,128]{3,2,1,0:T(8,128)(2,1)S(1)} %bitcast.58, f32[4,16,64,128]{3,2,1,0:T(8,128)S(1)} %collective-permute-done.3.rest_0_), custom_call_target="tpu_custom_call" | custom-call | flops 6000000000 | bytes 3200000 | tf_op jit(solution)/shard_map/pallas_call | solution.py:50
  51.4 2.0 %collective-permute-done.5 = bf16[1,16,64,128]{3,2,1,0:T(8,128)(2,1)S(1)} collective-permute-done((bf16[1,16,64,128]{3,2,1,0:T(8,128)(2,1)S(1)}, bf16[1,16,64,128]{3,2,1,0:T(8,128)(2,1)S(1)}, u32[]{:S(2)}, u32[]{:S(2)}) %collective-permute-start.5) | collective-permute-done | bytes 262176 | tf_op jit(solution)/shard_map/ppermute | solution.py:86
  53.6 3.1 %collective-permute-start.10 = (bf16[2,16,64,128]{3,2,1,0:T(8,128)(2,1)S(1)}, bf16[2,16,64,128]{3,2,1,0:T(8,128)(2,1)S(1)}, u32[]{:S(2)}, u32[]{:S(2)}) collective-permute-start(bf16[2,16,64,128]{3,2,1,0:T(8,128)(2,1)S(1)} %pad_maximum_fusion.1), channel_id=1, source_target_pairs={{0,224},{32,0},{64,32},{96,64},{128,96},{160,128},{192,160},{224,1... | collective-permute-start | bytes 1572872 | tf_op jit(solution)/shard_map/ppermute | solution.py:86
  56.8 5.7 %shard_map.87 = f32[4,16,64,128]{3,2,1,0:T(8,128)S(1)} custom-call(s32[4]{0:T(128)S(1)} %pad_add_fusion.4.targets, s32[320]{0:T(512)S(1)} %multiply_add_fusion.codes, bf16[8,64,256]{2,1,0:T(8,128)(2,1)S(1)} %all-to-all-done.columns, bf16[32,10,128,128]{3,2,1,0:T(8,128)(2,1)S(1)} %bitcast.59, f32[4,16,64,128]{3,2,1,0:T(8,128)S(1)} %collective-permute-done.2.rest_0_), custom_call_target="tpu_custom_call" | custom-call | flops 6000000000 | bytes 3200000 | tf_op jit(solution)/shard_map/pallas_call | solution.py:50
  62.5 5.0 %collective-permute-done.10 = bf16[2,16,64,128]{3,2,1,0:T(8,128)(2,1)S(1)} collective-permute-done((bf16[2,16,64,128]{3,2,1,0:T(8,128)(2,1)S(1)}, bf16[2,16,64,128]{3,2,1,0:T(8,128)(2,1)S(1)}, u32[]{:S(2)}, u32[]{:S(2)}) %collective-permute-start.10) | collective-permute-done | bytes 524320 | tf_op jit(solution)/shard_map/ppermute | solution.py:86
  67.5 3.5 %collective-permute-done.6 = bf16[2,16,64,128]{3,2,1,0:T(8,128)(2,1)S(1)} collective-permute-done((bf16[2,16,64,128]{3,2,1,0:T(8,128)(2,1)S(1)}, bf16[2,16,64,128]{3,2,1,0:T(8,128)(2,1)S(1)}, u32[]{:S(2)}, u32[]{:S(2)}) %collective-permute-start.6) | collective-permute-done | bytes 524320 | tf_op jit(solution)/shard_map/ppermute | solution.py:86
  73.5 6.1 %shard_map.85 = f32[4,16,64,128]{3,2,1,0:T(8,128)S(1)} custom-call(s32[4]{0:T(128)S(1)} %pad_add_fusion.2.targets, s32[320]{0:T(512)S(1)} %multiply_add_fusion.codes, bf16[8,64,256]{2,1,0:T(8,128)(2,1)S(1)} %all-to-all-done.columns, bf16[32,10,128,128]{3,2,1,0:T(8,128)(2,1)S(1)} %bitcast.60, f32[4,16,64,128]{3,2,1,0:T(8,128)S(1)} %collective-permute-done.1.rest_0_), custom_call_target="tpu_custom_call" | custom-call | flops 6000000000 | bytes 3200000 | tf_op jit(solution)/shard_map/pallas_call | solution.py:50
  79.6 4.0 %collective-permute-done.11 = bf16[2,16,64,128]{3,2,1,0:T(8,128)(2,1)S(1)} collective-permute-done((bf16[2,16,64,128]{3,2,1,0:T(8,128)(2,1)S(1)}, bf16[2,16,64,128]{3,2,1,0:T(8,128)(2,1)S(1)}, u32[]{:S(2)}, u32[]{:S(2)}) %collective-permute-start.11) | collective-permute-done | bytes 524320 | tf_op jit(solution)/shard_map/ppermute | solution.py:86
  88.5 4.0 %copy-done.2 = bf16[1,32,10,128,128]{4,3,2,1,0:T(8,128)(2,1)S(1)} copy-done((bf16[1,32,10,128,128]{4,3,2,1,0:T(8,128)(2,1)S(1)}, bf16[1,32,10,128,128]{4,3,2,1,0:T(8,128)(2,1)}, u32[]{:S(2)}) %copy-start.2) | copy-done | bytes 10485784
  94.2 3.7 %collective-permute-done.12 = bf16[2,16,64,128]{3,2,1,0:T(8,128)(2,1)S(1)} collective-permute-done((bf16[2,16,64,128]{3,2,1,0:T(8,128)(2,1)}, bf16[2,16,64,128]{3,2,1,0:T(8,128)(2,1)S(1)}, u32[]{:S(2)}, u32[]{:S(2)}) %collective-permute-start.12) | collective-permute-done | bytes 524320 | tf_op jit(solution)/shard_map/ppermute | solution.py:86
  100.8 6.3 %collective-permute-start.13 = (bf16[16,64,128]{2,1,0:T(8,128)(2,1)S(1)}, bf16[16,64,128]{2,1,0:T(8,128)(2,1)S(1)}, u32[]{:S(2)}, u32[]{:S(2)}) collective-permute-start(bf16[16,64,128]{2,1,0:T(8,128)(2,1)S(1)} %fusion.9), channel_id=1, source_target_pairs={{0,16},{16,0},{1,17},{17,1},{2,18},{18,2},{3,19},{19,3},{4,20},{20... | collective-permute-start | bytes 786440 | tf_op jit(solution)/shard_map/ppermute | solution.py:90
  107.1 4.3 %collective-permute-done.13 = bf16[16,64,128]{2,1,0:T(8,128)(2,1)S(1)} collective-permute-done((bf16[16,64,128]{2,1,0:T(8,128)(2,1)S(1)}, bf16[16,64,128]{2,1,0:T(8,128)(2,1)S(1)}, u32[]{:S(2)}, u32[]{:S(2)}) %collective-permute-start.13) | collective-permute-done | bytes 262176 | tf_op jit(solution)/shard_map/ppermute | solution.py:90
  112.2 5.1 %all-to-all-start.1 = ((bf16[8,2,64,128]{3,2,1,0:T(8,128)(2,1)}), bf16[8,2,64,128]{3,2,1,0:T(8,128)(2,1)S(1)}, u32[]{:S(2)}, u32[]{:S(2)}) async-start(bf16[8,2,64,128]{3,2,1,0:T(8,128)(2,1)} %bitcast.38), calls=%async_computation.1 | async-start | bytes 524288 | tf_op jit(solution)/shard_map/all_to_all | solution.py:145
  117.7 5.8 %all-to-all-done.1.neighbors = bf16[8,2,64,128]{3,2,1,0:T(8,128)(2,1)S(1)} async-done(((bf16[8,2,64,128]{3,2,1,0:T(8,128)(2,1)}), bf16[8,2,64,128]{3,2,1,0:T(8,128)(2,1)S(1)}, u32[]{:S(2)}, u32[]{:S(2)}) %all-to-all-start.1) | async-done | bytes 262176 | tf_op jit(solution)/shard_map/all_to_all | solution.py:145
  (69 shorter events, 22.2 us)
Async XLA Ops:
  0.0 117.3 %copy-start = (bf16[512,512]{1,0:T(8,128)(2,1)S(1)}, bf16[512,512]{1,0:T(8,128)(2,1)}, u32[]{:S(2)}) copy-start(bf16[512,512]{1,0:T(8,128)(2,1)} %param.14) | copy-start | bytes 1572868
  0.0 12.2 %all-to-all-start = ((bf16[8,64,256]{2,1,0:T(8,128)(2,1)}), bf16[8,64,256]{2,1,0:T(8,128)(2,1)S(1)}, u32[]{:S(2)}, u32[]{:S(2)}) async-start(bf16[8,64,256]{2,1,0:T(8,128)(2,1)} %bitcast.62), calls=%async_computation | async-start | bytes 524288 | tf_op jit(solution)/shard_map/all_to_all | solution.py:99
  20.8 21.0 %collective-permute-start.3 = (f32[4,16,64,128]{3,2,1,0:T(8,128)S(1)}, f32[4,16,64,128]{3,2,1,0:T(8,128)S(1)}, u32[]{:S(2)}, u32[]{:S(2)}) collective-permute-start(f32[4,16,64,128]{3,2,1,0:T(8,128)S(1)} %shard_map.88), channel_id=1, source_target_pairs={{0,8},{8,0},{1,9},{9,1},{2,10},{10,2},{3,11},{11,3},{4,12},{12,4},... | collective-permute-start | bytes 6291464 | tf_op jit(solution)/shard_map/ppermute | solution.py:90
  20.9 8.8 %slice-start = ((s8[10485760]{0:T(1024)(128)(4,1)}), s8[4194304]{0:T(1024)(128)(4,1)S(1)}, s32[]{:S(2)}) async-start(s8[10485760]{0:T(1024)(128)(4,1)} %bitcast.53), calls=%async_computation.2 | async-start | bytes 8388608
  20.9 8.8 %slice-start.1 = ((s8[10485760]{0:T(1024)(128)(4,1)}), s8[4194304]{0:T(1024)(128)(4,1)S(1)}, s32[]{:S(2)}) async-start(s8[10485760]{0:T(1024)(128)(4,1)} %bitcast.53), calls=%async_computation.3 | async-start | bytes 8388608
  23.2 6.5 %slice-start.2 = ((s8[10485760]{0:T(1024)(128)(4,1)}), s8[2097152]{0:T(1024)(128)(4,1)S(1)}, s32[]{:S(2)}) async-start(s8[10485760]{0:T(1024)(128)(4,1)} %bitcast.53), calls=%async_computation.4 | async-start | bytes 4194304
  23.2 16.2 %collective-permute-start.4 = (f32[2,16,64,128]{3,2,1,0:T(8,128)S(1)}, f32[2,16,64,128]{3,2,1,0:T(8,128)S(1)}, u32[]{:S(2)}, u32[]{:S(2)}) collective-permute-start(f32[2,16,64,128]{3,2,1,0:T(8,128)S(1)} %shard_map.90), channel_id=1, source_target_pairs={{0,8},{8,0},{1,9},{9,1},{2,10},{10,2},{3,11},{11,3},{4,12},{12,4},... | collective-permute-start | bytes 3145736 | tf_op jit(solution)/shard_map/ppermute | solution.py:90
  29.4 27.4 %collective-permute-start.2 = (f32[4,16,64,128]{3,2,1,0:T(8,128)S(1)}, f32[4,16,64,128]{3,2,1,0:T(8,128)S(1)}, u32[]{:S(2)}, u32[]{:S(2)}) collective-permute-start(f32[4,16,64,128]{3,2,1,0:T(8,128)S(1)} %shard_map.86), channel_id=1, source_target_pairs={{0,8},{8,0},{1,9},{9,1},{2,10},{10,2},{3,11},{11,3},{4,12},{12,4},... | collective-permute-start | bytes 6291464 | tf_op jit(solution)/shard_map/ppermute | solution.py:90
  34.1 39.4 %collective-permute-start.1 = (f32[4,16,64,128]{3,2,1,0:T(8,128)S(1)}, f32[4,16,64,128]{3,2,1,0:T(8,128)S(1)}, u32[]{:S(2)}, u32[]{:S(2)}) collective-permute-start(f32[4,16,64,128]{3,2,1,0:T(8,128)S(1)} %shard_map.84), channel_id=1, source_target_pairs={{0,8},{8,0},{1,9},{9,1},{2,10},{10,2},{3,11},{11,3},{4,12},{12,4},... | collective-permute-start | bytes 6291464 | tf_op jit(solution)/shard_map/ppermute | solution.py:90
  39.1 49.4 %collective-permute-start = (f32[2,16,64,128]{3,2,1,0:T(8,128)S(1)}, f32[2,16,64,128]{3,2,1,0:T(8,128)S(1)}, u32[]{:S(2)}, u32[]{:S(2)}) collective-permute-start(f32[2,16,64,128]{3,2,1,0:T(8,128)S(1)} %shard_map.82), channel_id=1, source_target_pairs={{0,8},{8,0},{1,9},{9,1},{2,10},{10,2},{3,11},{11,3},{4,12},{12,4},... | collective-permute-start | bytes 3145736 | tf_op jit(solution)/shard_map/ppermute | solution.py:90
  41.7 11.6 %collective-permute-start.5 = (bf16[1,16,64,128]{3,2,1,0:T(8,128)(2,1)S(1)}, bf16[1,16,64,128]{3,2,1,0:T(8,128)(2,1)S(1)}, u32[]{:S(2)}, u32[]{:S(2)}) collective-permute-start(bf16[1,16,64,128]{3,2,1,0:T(8,128)(2,1)S(1)} %get-tuple-element.13), channel_id=1, source_target_pairs={{0,32},{32,64},{64,96},{96,128},{128,160},{160,192},{192,224},{224... | collective-permute-start | bytes 786440 | tf_op jit(solution)/shard_map/ppermute | solution.py:86
  41.8 11.5 %collective-permute-start.9 = (bf16[1,16,64,128]{3,2,1,0:T(8,128)(2,1)S(1)}, bf16[1,16,64,128]{3,2,1,0:T(8,128)(2,1)S(1)}, u32[]{:S(2)}, u32[]{:S(2)}) collective-permute-start(bf16[1,16,64,128]{3,2,1,0:T(8,128)(2,1)S(1)} %get-tuple-element.14), channel_id=1, source_target_pairs={{0,224},{32,0},{64,32},{96,64},{128,96},{160,128},{192,160},{224,1... | collective-permute-start | bytes 786440 | tf_op jit(solution)/shard_map/ppermute | solution.py:86
  53.6 13.9 %collective-permute-start.10 = (bf16[2,16,64,128]{3,2,1,0:T(8,128)(2,1)S(1)}, bf16[2,16,64,128]{3,2,1,0:T(8,128)(2,1)S(1)}, u32[]{:S(2)}, u32[]{:S(2)}) collective-permute-start(bf16[2,16,64,128]{3,2,1,0:T(8,128)(2,1)S(1)} %pad_maximum_fusion.1), channel_id=1, source_target_pairs={{0,224},{32,0},{64,32},{96,64},{128,96},{160,128},{192,160},{224,1... | collective-permute-start | bytes 1572872 | tf_op jit(solution)/shard_map/ppermute | solution.py:86
  56.7 14.3 %collective-permute-start.6 = (bf16[2,16,64,128]{3,2,1,0:T(8,128)(2,1)S(1)}, bf16[2,16,64,128]{3,2,1,0:T(8,128)(2,1)S(1)}, u32[]{:S(2)}, u32[]{:S(2)}) collective-permute-start(bf16[2,16,64,128]{3,2,1,0:T(8,128)(2,1)S(1)} %pad_maximum_fusion), channel_id=1, source_target_pairs={{0,32},{32,64},{64,96},{96,128},{128,160},{160,192},{192,224},{224... | collective-permute-start | bytes 1572872 | tf_op jit(solution)/shard_map/ppermute | solution.py:86
  71.4 12.2 %collective-permute-start.11 = (bf16[2,16,64,128]{3,2,1,0:T(8,128)(2,1)S(1)}, bf16[2,16,64,128]{3,2,1,0:T(8,128)(2,1)S(1)}, u32[]{:S(2)}, u32[]{:S(2)}) collective-permute-start(bf16[2,16,64,128]{3,2,1,0:T(8,128)(2,1)S(1)} %get-tuple-element.8), channel_id=1, source_target_pairs={{0,224},{32,0},{64,32},{96,64},{128,96},{160,128},{192,160},{224,1... | collective-permute-start | bytes 1572872 | tf_op jit(solution)/shard_map/ppermute | solution.py:86
  71.6 13.5 %collective-permute-start.7 = (bf16[2,16,64,128]{3,2,1,0:T(8,128)(2,1)S(1)}, bf16[2,16,64,128]{3,2,1,0:T(8,128)(2,1)S(1)}, u32[]{:S(2)}, u32[]{:S(2)}) collective-permute-start(bf16[2,16,64,128]{3,2,1,0:T(8,128)(2,1)S(1)} %get-tuple-element.7), channel_id=1, source_target_pairs={{0,32},{32,64},{64,96},{96,128},{128,160},{160,192},{192,224},{224... | collective-permute-start | bytes 1572872 | tf_op jit(solution)/shard_map/ppermute | solution.py:86
  86.4 11.5 %collective-permute-start.12 = (bf16[2,16,64,128]{3,2,1,0:T(8,128)(2,1)}, bf16[2,16,64,128]{3,2,1,0:T(8,128)(2,1)S(1)}, u32[]{:S(2)}, u32[]{:S(2)}) collective-permute-start(bf16[2,16,64,128]{3,2,1,0:T(8,128)(2,1)} %get-tuple-element.6), channel_id=1, source_target_pairs={{0,224},{32,0},{64,32},{96,64},{128,96},{160,128},{192,160},{224,1... | collective-permute-start | bytes 1572872 | tf_op jit(solution)/shard_map/ppermute | solution.py:86
  86.6 12.8 %collective-permute-start.8 = (bf16[2,16,64,128]{3,2,1,0:T(8,128)(2,1)}, bf16[2,16,64,128]{3,2,1,0:T(8,128)(2,1)}, u32[]{:S(2)}, u32[]{:S(2)}) collective-permute-start(bf16[2,16,64,128]{3,2,1,0:T(8,128)(2,1)} %get-tuple-element.5), channel_id=1, source_target_pairs={{0,32},{32,64},{64,96},{96,128},{128,160},{160,192},{192,224},{224... | collective-permute-start | bytes 1572872 | tf_op jit(solution)/shard_map/ppermute | solution.py:86
  88.5 4.0 %copy-start.2 = (bf16[1,32,10,128,128]{4,3,2,1,0:T(8,128)(2,1)S(1)}, bf16[1,32,10,128,128]{4,3,2,1,0:T(8,128)(2,1)}, u32[]{:S(2)}) copy-start(bf16[1,32,10,128,128]{4,3,2,1,0:T(8,128)(2,1)} %param.9) | copy-start | bytes 31457284
  94.2 12.9 %copy-start.5 = (s32[2048]{0:T(1024)S(1)}, s32[2048]{0:T(1024)}, u32[]{:S(2)}) copy-start(s32[2048]{0:T(1024)} %param.13) | copy-start | bytes 24580
  94.2 23.1 %copy-start.4 = (bf16[512,256]{1,0:T(8,128)(2,1)S(1)}, bf16[512,256]{1,0:T(8,128)(2,1)}, u32[]{:S(2)}) copy-start(bf16[512,256]{1,0:T(8,128)(2,1)} %param.8) | copy-start | bytes 786436
  100.7 22.8 %copy-start.3 = (bf16[512,512]{1,0:T(8,128)(2,1)S(1)}, bf16[512,512]{1,0:T(8,128)(2,1)}, u32[]{:S(2)}) copy-start(bf16[512,512]{1,0:T(8,128)(2,1)} %weight.1) | copy-start | bytes 1572868
  100.8 10.7 %collective-permute-start.13 = (bf16[16,64,128]{2,1,0:T(8,128)(2,1)S(1)}, bf16[16,64,128]{2,1,0:T(8,128)(2,1)S(1)}, u32[]{:S(2)}, u32[]{:S(2)}) collective-permute-start(bf16[16,64,128]{2,1,0:T(8,128)(2,1)S(1)} %fusion.9), channel_id=1, source_target_pairs={{0,16},{16,0},{1,17},{17,1},{2,18},{18,2},{3,19},{19,3},{4,20},{20... | collective-permute-start | bytes 786440 | tf_op jit(solution)/shard_map/ppermute | solution.py:90
  112.2 11.2 %all-to-all-start.1 = ((bf16[8,2,64,128]{3,2,1,0:T(8,128)(2,1)}), bf16[8,2,64,128]{3,2,1,0:T(8,128)(2,1)S(1)}, u32[]{:S(2)}, u32[]{:S(2)}) async-start(bf16[8,2,64,128]{3,2,1,0:T(8,128)(2,1)} %bitcast.38), calls=%async_computation.1 | async-start | bytes 524288 | tf_op jit(solution)/shard_map/all_to_all | solution.py:145
  (1 other events, 4.0 us)
